TPU v7x, 256 devices: a whole 4x4x8 slice. The times are simulated.
256 devices in a mesh: dp: 8 (over z_lo, core), seq: 16 (over x, y), mp: 2 (over z_hi).
Axes of the slice: x: 4, y: 4, z: 8 (z_hi: 2, z_lo: 4; z = z_hi * 4 + z_lo), core: 2. Of those that a mesh axis runs over, the one named last changes fastest.
Arguments:
- features: bfloat16 [8, 8192, 1408], P('dp', ('seq', 'mp')), may hold values from -6 to 6
- conv_weight: bfloat16 [5, 1408, 1536], P(None, ('seq', 'mp')), may hold values from -0.0625 to 0.0625
- norm_gain: float32 [1536], replicated, may hold values from 0.25 to 1.75
- query_weight: bfloat16 [1536, 1024], replicated, may hold values from -0.15625 to 0.15625
- keyval_weight: bfloat16 [1536, 320], replicated, may hold values from -0.15625 to 0.15625
- head_scale: float32 [8], replicated, may hold values from 0.5 to 24
- output_weight: bfloat16 [1536, 1536], replicated, may hold values from -0.15625 to 0.15625
- pair_weight: bfloat16 [1536, 256], replicated, may hold values from -0.625 to 0.625
- pair_input: bfloat16 [8, 256, 256, 128], P('dp', ('seq', 'mp')), may hold values from -6 to 6
- flip_weight: bfloat16 [128, 128], replicated, may hold values from -0.5 to 0.5
- pair_cotangent: bfloat16 [8, 256, 256, 128], P('dp', ('seq', 'mp')), may hold values from -0.0234375 to 0.0234375
Outputs:
- block_out: bfloat16 [8, 4096, 1536], P('dp', ('seq', 'mp'))
- pair_out: bfloat16 [8, 256, 256, 128], P('dp', ('seq', 'mp'))
- grad_flip: float32 [128, 128], replicated
All inputs are finite; a program needn't handle non-finite values.
Results may differ from a plain program's by a relative error of at most 0.011.
Values may be sent and summed in bfloat16 or wider, within the bound.
A program may use at most 192 MiB of HBM per device.

v0:
```python
import math
import jax
import jax.numpy as jnp
from jax import lax
from jax.sharding import PartitionSpec as P

PAIR_POOL = 16
norm_eps = 1e-06
logit_cap = 50.0


def padded_2(shard, sides, width):
    for axis, dim in sides:
        devices, length = (lax.axis_size(axis), shard.shape[dim])
        up = [(i, (i + 1) % devices) for i in range(devices - 1)]
        down = [(j, i) for i, j in up]
        last = lax.slice_in_dim(shard, length - width, length, axis=dim)
        initial = lax.slice_in_dim(shard, 0, width, axis=dim)
        before = lax.ppermute(last, axis, up)
        after = lax.ppermute(initial, axis, down)
        shard = jnp.concatenate([before, shard, after], axis=dim)
    return shard


def root_norm(values_in):
    return values_in * lax.rsqrt(jnp.mean(values_in * values_in, axis=-1, keepdims=True) + norm_eps)


def prepare(raw):
    return jax.nn.gelu(root_norm(raw.astype(jnp.float32)), approximate=False).astype(jnp.bfloat16)


def tap_sum(source, out_rows, tap_count, running, filter_rows):
    for lag_index in range(tap_count):
        running = running + jnp.dot(
            source[lag_index : lag_index + out_rows],
            filter_rows[lag_index],
            preferred_element_type=jnp.float32,
        )
    return running


def per_device(
    features,
    conv_weight,
    norm_gain,
    query_weight,
    keyval_weight,
    head_scale,
    output_weight,
    pair_weight,
    pair_input,
    flip_weight,
    pair_cotangent,
):
    fine_rows = features.shape[1]
    coarse_rows = fine_rows // 2
    in_channels = features.shape[2]
    model_dim = output_weight.shape[1]
    head_count = head_scale.shape[0]
    key_dim = query_weight.shape[1] // head_count
    pair_dim = flip_weight.shape[0]
    tap_count = conv_weight.shape[0]
    margin = tap_count // 2
    padded = padded_2(features, ((("seq", "mp"), 1),), margin)
    prepared = prepare(padded[0])
    starting = jnp.zeros((fine_rows, model_dim), jnp.float32)
    conv_sum = tap_sum(
        prepared,
        fine_rows,
        tap_count,
        starting,
        lax.all_gather(conv_weight, ("seq", "mp"), axis=1, tiled=True),
    )
    skipped = jnp.pad(features[0].astype(jnp.float32), ((0, 0), (0, model_dim - in_channels)))
    encoded = jnp.max((conv_sum + skipped).reshape(coarse_rows, 2, model_dim), axis=1).astype(
        jnp.bfloat16
    )
    widened = encoded.astype(jnp.float32)
    normed = (root_norm(widened) * norm_gain).astype(jnp.bfloat16)
    scale_row = jnp.repeat(head_scale, key_dim) / math.sqrt(key_dim)
    queries = (
        jnp.dot(normed, query_weight, preferred_element_type=jnp.float32) * scale_row
    ).astype(jnp.bfloat16)
    keyvals = jnp.dot(normed, keyval_weight, preferred_element_type=jnp.float32).astype(
        jnp.bfloat16
    )
    pooled = jnp.mean(
        widened.reshape(coarse_rows // PAIR_POOL, PAIR_POOL, model_dim), axis=1
    ).astype(jnp.bfloat16)
    pair_feats = jnp.dot(pooled, pair_weight, preferred_element_type=jnp.float32).astype(
        jnp.bfloat16
    )
    pair_q = pair_feats[:, :pair_dim]
    pair_k = pair_feats[:, pair_dim:]
    keys_all, pairk_all = (
        lax.all_gather(keyvals[None], ("seq", "mp"), axis=1, tiled=True),
        lax.all_gather(pair_k[None], ("seq", "mp"), axis=1, tiled=True),
    )
    summed = (
        pair_input[0].astype(jnp.float32)
        + pair_q[:, None, :].astype(jnp.float32) * pairk_all[0][None, :, :].astype(jnp.float32)
    ).astype(jnp.bfloat16)
    flipped = lax.all_to_all(summed[None], ("seq", "mp"), split_axis=2, concat_axis=1, tiled=True)[
        0
    ]
    turned = jnp.einsum("bac,cd->abd", flipped, flip_weight, preferred_element_type=jnp.float32)
    pair_out = (summed.astype(jnp.float32) + turned).astype(jnp.bfloat16)
    grad_term = jnp.einsum(
        "bac,abd->cd", flipped, pair_cotangent[0], preferred_element_type=jnp.float32
    )
    grad_flip = lax.psum(grad_term, ("dp", "seq", "mp"))
    key_rows = keys_all[0][:, :key_dim]
    value_rows = keys_all[0][:, key_dim:]
    query_rows = queries.reshape(coarse_rows * head_count, key_dim)
    scores = jnp.dot(query_rows, key_rows.T, preferred_element_type=jnp.float32)
    weights = jnp.exp(logit_cap * jnp.tanh(scores / logit_cap))
    totals = jnp.sum(weights, axis=-1, keepdims=True)
    mixed = (
        jnp.dot(weights.astype(jnp.bfloat16), value_rows, preferred_element_type=jnp.float32)
        / totals
    )
    heads_out = mixed.astype(jnp.bfloat16).reshape(coarse_rows, head_count * value_rows.shape[1])
    block_out = (
        widened + jnp.dot(heads_out, output_weight, preferred_element_type=jnp.float32)
    ).astype(jnp.bfloat16)
    return (block_out[None], pair_out[None], grad_flip)


def solution(mesh):
    placed = (
        P("dp", ("seq", "mp"), None),
        P(None, ("seq", "mp"), None),
        P(),
        P(),
        P(),
        P(),
        P(),
        P(),
        P("dp", ("seq", "mp"), None, None),
        P(),
        P("dp", ("seq", "mp"), None, None),
    )
    return jax.shard_map(
        per_device,
        mesh=mesh,
        in_specs=placed,
        out_specs=(P("dp", ("seq", "mp"), None), P("dp", ("seq", "mp"), None, None), P()),
        check_vma=False,
    )
```

profile of v0, /device:TPU:1, one launch (start us, length us, event | category | flops | bytes accessed | tf_op | source)
XLA Modules:
  0.0 959.2 jit_solution(9439417309653292819)
XLA Ops:
  7.2 2.7 copy.24
  12.0 10.3 %collective-permute-start = (bf16[1,2,1408]{2,1,0:T(2,128)(2,1)S(1)}, bf16[1,2,1408]{2,1,0:T(2,128)(2,1)S(1)}, u32[]{:S(2)}, u32[]{:S(2)}) collective-permute-start(bf16[1,2,1408]{2,1,0:T(2,128)(2,1)S(1)} %get-tuple-element.8), channel_id=1, source_target_pairs={{0,1},{1,2},{2,3},{3,4},{4,5},{5,6},{6,7},{7,8},{8,9},{9,10},{10,1... | collective-permute-start | bytes 16904 | tf_op jit(solution)/shard_map/ppermute | solution.py:19
  24.5 6.0 fusion.20
  30.5 426.3 %all-gather.5.cloned.1.call-done = bf16[5,1408,1536]{2,0,1:T(8,128)(2,1)} async-done(((bf16[5,44,1536]{2,0,1:T(8,128)(2,1)}), bf16[5,1408,1536]{2,0,1:T(8,128)(2,1)}) %all-gather.5.cloned.1.call-update) | async-done | bytes 21626896 | tf_op jit(solution)/shard_map/all_gather | solution.py:73
  456.8 92.6 %fusion.83 = (bf16[1,1408,1536]{2,0,1:T(2,128)(2,1)S(1)}, bf16[1,1408,1536]{2,0,1:T(2,128)(2,1)S(1)}, bf16[1,1408,1536]{2,0,1:T(2,128)(2,1)}, bf16[1,1408,1536]{2,0,1:T(2,128)(2,1)}, bf16[1,1408,1536]{2,0,1:T(2,128)(2,1)}) fusion(bf16[5,1408,1536]{2,0,1:T(8,128)(2,1)} %all-gather.5.cloned.1.call-done), kind=kLoop, calls=%fused_computation.101 | loop fusion | bytes 43253760 | tf_op jit(solution)/shard_map/slice | solution.py:37
  549.4 5.0 fusion.7
  554.5 4.9 fusion.9
  562.3 2.3 fusion.13
  564.6 2.9 reshape.58
  567.5 3.0 reduce_max.9
  570.7 2.3 convolution_convert_fusion
  574.6 105.2 %all-gather.1 = bf16[256,128]{1,0:T(8,128)(2,1)S(1)} all-gather(bf16[8,128]{1,0:T(8,128)(2,1)S(1)} %get-tuple-element.11), channel_id=3, replica_groups=mesh['dp'=8,'seq'=16,'mp'=2] {'seq','mp'}, dimensions={0}, use_global_device_ids=true | all-gather | bytes 67584 | tf_op jit(solution)/shard_map/all_gather | solution.py:98
  681.6 4.6 all-to-all-start
  688.3 1.8 reshape.59
  690.1 9.7 %all-to-all-done = bf16[1,8,256,128]{3,1,0,2:T(8,128)(2,1)} async-done(((bf16[1,8,256,128]{3,1,0,2:T(8,128)(2,1)}), bf16[1,8,256,128]{3,1,0,2:T(8,128)(2,1)}, u32[]{:S(2)}, u32[]{:S(2)}) %all-to-all-start) | async-done | bytes 524320 | tf_op jit(solution)/shard_map/all_to_all | solution.py:104
  699.8 2.2 convolution_bitcast_fusion.1
  702.0 2.3 fusion.51
  704.4 6.7 fusion
  711.1 5.9 fusion.63
  717.0 2.0 copy.30
  719.0 2.3 reshape.60
  721.3 4.0 fusion.15
  725.3 225.9 %all-reduce.3.cloned.1.call-done = f32[128,128]{1,0:T(8,128)} async-done(((f32[128,128]{1,0:T(8,128)}), f32[128,128]{1,0:T(8,128)}) %all-reduce.3.cloned.1.call-update) | async-done | bytes 65552 | tf_op jit(solution)/shard_map/psum | solution.py:112
  951.2 1.5 copy.69
  (47 shorter events, 12.8 us)
Async XLA Ops:
  7.2 679.8 %copy-start = (bf16[1536,1024]{1,0:T(8,128)(2,1)S(1)}, bf16[1536,1024]{1,0:T(8,128)(2,1)}, u32[]{:S(2)}) copy-start(bf16[1536,1024]{1,0:T(8,128)(2,1)} %param.14) | copy-start | bytes 9437188
  7.2 449.6 %all-gather.5.cloned.1.call-start = ((), (), s32[]{:S(2)}) async-start(), calls=%async_computation.1 | async-start | bytes 35684352 | tf_op jit(solution)/shard_map/all_gather | solution.py:73
  9.9 694.5 %all-gather.7.cloned.1.call-start = ((), (), s32[]{:S(2)}) async-start(), calls=%async_computation.3 | async-start | bytes 2703360 | tf_op jit(solution)/shard_map/all_gather | solution.py:97
  10.7 11.6 %collective-permute-start.1 = (bf16[1,2,1408]{2,1,0:T(2,128)(2,1)S(1)}, bf16[1,2,1408]{2,1,0:T(2,128)(2,1)S(1)}, u32[]{:S(2)}, u32[]{:S(2)}) collective-permute-start(bf16[1,2,1408]{2,1,0:T(2,128)(2,1)S(1)} %get-tuple-element.9), channel_id=1, source_target_pairs={{1,0},{2,1},{3,2},{4,3},{5,4},{6,5},{7,6},{8,7},{9,8},{10,9},{11,1... | collective-permute-start | bytes 16904 | tf_op jit(solution)/shard_map/ppermute | solution.py:20
  12.0 11.0 %collective-permute-start = (bf16[1,2,1408]{2,1,0:T(2,128)(2,1)S(1)}, bf16[1,2,1408]{2,1,0:T(2,128)(2,1)S(1)}, u32[]{:S(2)}, u32[]{:S(2)}) collective-permute-start(bf16[1,2,1408]{2,1,0:T(2,128)(2,1)S(1)} %get-tuple-element.8), channel_id=1, source_target_pairs={{0,1},{1,2},{2,3},{3,4},{4,5},{5,6},{6,7},{7,8},{8,9},{9,10},{10,1... | collective-permute-start | bytes 16904 | tf_op jit(solution)/shard_map/ppermute | solution.py:19
  456.8 92.6 %copy-start.4 = (bf16[260,1408]{1,0:T(8,128)(2,1)S(1)}, bf16[260,1408]{1,0:T(8,128)(2,1)}, u32[]{:S(2)}) copy-start(bf16[260,1408]{1,0:T(8,128)(2,1)} %fusion.20) | copy-start | bytes 2196484
  549.4 9.9 %slice-start = ((s8[8650752]{0:T(1024)(128)(4,1)}), s8[4194304]{0:T(1024)(128)(4,1)S(1)}, s32[]{:S(2)}) async-start(s8[8650752]{0:T(1024)(128)(4,1)} %bitcast.79), calls=%async_computation.4 | async-start | bytes 8388608
  549.4 9.9 %slice-start.1 = ((s8[8650752]{0:T(1024)(128)(4,1)}), s8[4194304]{0:T(1024)(128)(4,1)S(1)}, s32[]{:S(2)}) async-start(s8[8650752]{0:T(1024)(128)(4,1)} %bitcast.79), calls=%async_computation.5 | async-start | bytes 8388608
  554.4 4.9 slice-start.2
  560.8 1.4 copy-start.1
  564.6 6.1 copy-start.5
  573.0 106.8 %copy-start.2 = (bf16[1,8,256,128]{3,2,1,0:T(8,128)(2,1)S(1)}, bf16[1,8,256,128]{3,2,1,0:T(8,128)(2,1)}, u32[]{:S(2)}) copy-start(bf16[1,8,256,128]{3,2,1,0:T(8,128)(2,1)} %param.19) | copy-start | bytes 1572868
  679.8 0.6 copy-start.3
  681.6 18.2 %all-to-all-start = ((bf16[1,8,256,128]{3,1,0,2:T(8,128)(2,1)}), bf16[1,8,256,128]{3,1,0,2:T(8,128)(2,1)}, u32[]{:S(2)}, u32[]{:S(2)}) async-start(bf16[1,8,256,128]{3,1,0,2:T(8,128)(2,1)} %copy.31), calls=%async_computation | async-start | bytes 1048576 | tf_op jit(solution)/shard_map/all_to_all | solution.py:104
  686.2 264.9 %all-reduce.3.cloned.1.call-start = ((), (), s32[]{:S(2)}) async-start(), calls=%async_computation.2 | async-start | bytes 131072 | tf_op jit(solution)/shard_map/psum | solution.py:112
  704.4 6.7 copy-start.6
Sparse Core Ops, SparseCore 0:
  11.4 445.3 all-gather.4
  573.2 103.0 all-gather.6
  704.5 246.6 all-reduce.2
where the time goes:
time: 960 us; the launch traced here: 959 us
  waiting for transfers between devices  663 us (69%)
  local copies, waits for them, and re-layouts  108 us (11%)
  blocking collectives  105 us (11%)
  matrix products  41.2 us (4%)
  starting transfers between devices  16.3 us (2%)
  between operations  14 us (1%)
  other arithmetic  11.6 us (1%)
    all_gather x1, waiting for transfers between devices, per_device(): lax.all_gather(conv_weight, ('seq', 'mp'), axis=1, tiled=True)  426 us
    psum x1, waiting for transfers between devices, per_device(): grad_flip = lax.psum(grad_term, ('dp', 'seq', 'mp'))  226 us
    all_gather x1, blocking collectives, per_device(): lax.all_gather(pair_k[None], ('seq', 'mp'), axis=1, tiled=True)  105 us
    slice x1, local copies, waits for them, and re-layouts, tap_sum(): filter_rows[lag_index]  92.6 us
  transfers between devices with their start and end apart: 6, of which 4 were waited for; matrix products, arithmetic and copies ran while one was open for 4% of the time, Pallas kernels for 0%

commit v1 on v0

--- a/solution.py
+++ b/solution.py
@@ -1,3 +1,4 @@
+import functools
 import math
 import jax
 import jax.numpy as jnp
@@ -7,6 +8,13 @@
 PAIR_POOL = 16
 norm_eps = 1e-06
 logit_cap = 50.0
+
+
+def _scan_packet(block_in, which_axis):
+    return jnp.sum(lax.all_gather(block_in, which_axis), axis=0)
+
+
+create_the_lines = functools.partial(_scan_packet, which_axis=("dp", "seq", "mp"))
 
 
 def padded_2(shard, sides, width):
@@ -109,7 +117,7 @@
     grad_term = jnp.einsum(
         "bac,abd->cd", flipped, pair_cotangent[0], preferred_element_type=jnp.float32
     )
-    grad_flip = lax.psum(grad_term, ("dp", "seq", "mp"))
+    grad_flip = create_the_lines(grad_term)
     key_rows = keys_all[0][:, :key_dim]
     value_rows = keys_all[0][:, key_dim:]
     query_rows = queries.reshape(coarse_rows * head_count, key_dim)

time: 960 us -> 1460 us (1.52)
  waiting for transfers between devices: 663 us -> 1140 us
  blocking collectives: 105 us -> 125 us
    all_gather x0 -> x1, waiting for transfers between devices: none -> 713 us  [_scan_packet(): return jnp.sum(lax.all_gather(block_in, which_axis), axis=0)]
    psum x1 -> x0, waiting for transfers between devices: 226 us -> none  [per_device(): grad_flip = lax.psum(grad_term, ('dp', 'seq', 'mp'))]
    all_to_all x0 -> x1, blocking collectives: none -> 16.6 us  [per_device(): lax.all_to_all(summed[None], ('seq', 'mp'), split_axis=2, concat_axis=1,...]
  transfers between devices with their start and end apart: 6 -> 5, of which waited for: 4 -> 3; matrix products, arithmetic and copies ran while one was open for 4% -> 3% of each run, Pallas kernels for 0% -> 0%
where the time goes in v1:
time: 1460 us
  waiting for transfers between devices  1140 us (78%)
  blocking collectives  125 us (9%)
  local copies, waits for them, and re-layouts  106 us (7%)
  matrix products  40 us (3%)
  other arithmetic  18.8 us (1%)
    all_gather x1, waiting for transfers between devices, _scan_packet(): return jnp.sum(lax.all_gather(block_in, which_axis), axis=0)  713 us
    all_gather x1, waiting for transfers between devices, per_device(): lax.all_gather(conv_weight, ('seq', 'mp'), axis=1, tiled=True)  426 us
    all_gather x1, blocking collectives, per_device(): lax.all_gather(pair_k[None], ('seq', 'mp'), axis=1, tiled=True)  108 us
    slice x1, local copies, waits for them, and re-layouts, tap_sum(): filter_rows[lag_index]  92.6 us
  transfers between devices with their start and end apart: 5, of which 3 were waited for; matrix products, arithmetic and copies ran while one was open for 3% of the time, Pallas kernels for 0%

profile of v1, /device:TPU:1, one launch (start us, length us, event | category | flops | bytes accessed | tf_op | source)
XLA Modules:
  0.0 1455.5 jit_solution(18303395627275141844)
XLA Ops:
  7.2 2.7 copy.24
  12.0 10.3 collective-permute-start
  23.1 1.4 fusion.48
  24.5 6.0 fusion.20
  30.5 426.3 %all-gather.7.cloned.1.call-done = bf16[5,1408,1536]{2,0,1:T(8,128)(2,1)} async-done(((bf16[5,44,1536]{2,0,1:T(8,128)(2,1)}), bf16[5,1408,1536]{2,0,1:T(8,128)(2,1)}) %all-gather.7.cloned.1.call-update) | async-done | bytes 21626896 | tf_op jit(solution)/shard_map/all_gather | solution.py:81
  456.8 92.6 %fusion.83 = (bf16[1,1408,1536]{2,0,1:T(2,128)(2,1)S(1)}, bf16[1,1408,1536]{2,0,1:T(2,128)(2,1)S(1)}, bf16[1,1408,1536]{2,0,1:T(2,128)(2,1)}, bf16[1,1408,1536]{2,0,1:T(2,128)(2,1)}, bf16[1,1408,1536]{2,0,1:T(2,128)(2,1)}) fusion(bf16[5,1408,1536]{2,0,1:T(8,128)(2,1)} %all-gather.7.cloned.1.call-done), kind=kLoop, calls=%fused_computation.101 | loop fusion | bytes 43253760 | tf_op jit(solution)/shard_map/slice | solution.py:45
  549.4 5.0 fusion.7
  554.5 4.9 fusion.9
  560.8 1.4 fusion.11
  562.3 2.3 fusion.13
  564.6 2.9 reshape.58
  567.5 3.0 reduce_max.9
  570.7 2.3 convolution_convert_fusion
  574.6 108.1 %all-gather.1 = bf16[256,128]{1,0:T(8,128)(2,1)S(1)} all-gather(bf16[8,128]{1,0:T(8,128)(2,1)S(1)} %get-tuple-element.11), channel_id=3, replica_groups=mesh['dp'=8,'seq'=16,'mp'=2] {'seq','mp'}, dimensions={0}, use_global_device_ids=true | all-gather | bytes 67584 | tf_op jit(solution)/shard_map/all_gather | solution.py:106
  683.3 16.6 %all_to_all.15 = bf16[1,8,256,128]{3,1,0,2:T(8,128)(2,1)S(1)} all-to-all(bf16[1,8,256,128]{3,1,0,2:T(8,128)(2,1)S(1)} %copy.31), channel_id=1, replica_groups=mesh['dp'=8,'seq'=16,'mp'=2] {'seq','mp'}, dimensions={2} | all-to-all | bytes 1048576 | tf_op jit(solution)/shard_map/all_to_all | solution.py:112
  703.8 1.8 reshape.59
  705.5 2.3 fusion.51
  707.9 6.7 fusion
  714.6 5.9 fusion.63
  720.5 2.0 copy.30
  722.5 2.3 reshape.60
  724.8 4.0 fusion.15
  728.8 713.0 %all-gather.11.cloned.1.call-done = f32[32768,128]{1,0:T(8,128)} async-done(((f32[128,128]{1,0:T(8,128)}), f32[32768,128]{1,0:T(8,128)}) %all-gather.11.cloned.1.call-update) | async-done | bytes 16777232 | tf_op jit(solution)/shard_map/all_gather | solution.py:14
  1441.8 7.2 reduce_sum.49
  (50 shorter events, 10.5 us)
Async XLA Ops:
  7.2 695.3 %copy-start = (bf16[1536,1024]{1,0:T(8,128)(2,1)S(1)}, bf16[1536,1024]{1,0:T(8,128)(2,1)}, u32[]{:S(2)}) copy-start(bf16[1536,1024]{1,0:T(8,128)(2,1)} %param.14) | copy-start | bytes 9437188
  7.2 449.6 %all-gather.7.cloned.1.call-start = ((), (), s32[]{:S(2)}) async-start(), calls=%async_computation.1 | async-start | bytes 35684352 | tf_op jit(solution)/shard_map/all_gather | solution.py:81
  9.9 698.0 %all-gather.9.cloned.1.call-start = ((), (), s32[]{:S(2)}) async-start(), calls=%async_computation.2 | async-start | bytes 2703360 | tf_op jit(solution)/shard_map/all_gather | solution.py:105
  10.7 11.6 collective-permute-start.1
  12.0 11.0 collective-permute-start
  456.8 92.6 %copy-start.5 = (bf16[260,1408]{1,0:T(8,128)(2,1)S(1)}, bf16[260,1408]{1,0:T(8,128)(2,1)}, u32[]{:S(2)}) copy-start(bf16[260,1408]{1,0:T(8,128)(2,1)} %fusion.20) | copy-start | bytes 2196484
  549.4 9.9 slice-start
  549.4 9.9 slice-start.1
  554.4 4.9 slice-start.2
  560.8 1.4 copy-start.2
  564.6 6.1 copy-start.7
  573.0 868.7 %all-gather.11.cloned.1.call-start = ((), (), s32[]{:S(2)}) async-start(), calls=%async_computation.3 | async-start | bytes 16842752 | tf_op jit(solution)/shard_map/all_gather | solution.py:14
  573.1 109.7 %copy-start.3 = (bf16[1,8,256,128]{3,2,1,0:T(8,128)(2,1)S(1)}, bf16[1,8,256,128]{3,2,1,0:T(8,128)(2,1)}, u32[]{:S(2)}) copy-start(bf16[1,8,256,128]{3,2,1,0:T(8,128)(2,1)} %param.19) | copy-start | bytes 1572868
  682.7 17.2 %copy-start.4 = (f32[256,128]{1,0:T(8,128)}, f32[256,128]{1,0:T(8,128)S(1)}, u32[]{:S(2)}) copy-start(f32[256,128]{1,0:T(8,128)S(1)} %mul.112) | copy-start | bytes 393220
  682.7 18.0 %copy-start.6 = (bf16[1,8,256,128]{3,2,1,0:T(8,128)(2,1)S(1)}, bf16[1,8,256,128]{3,2,1,0:T(8,128)(2,1)}, u32[]{:S(2)}) copy-start(bf16[1,8,256,128]{3,2,1,0:T(8,128)(2,1)} %param.21) | copy-start | bytes 1572868
  699.9 0.8 copy-start.1
  707.9 6.7 copy-start.8
Sparse Core Ops, SparseCore 0:
  11.4 445.3 all-gather.6
  573.2 104.7 all-gather.8
  701.8 739.8 all-gather.10
